TPU v7x, 32 devices: a whole 2x2x4 slice. The times are simulated.
32 devices in a mesh: dp: 4 (over z), mp: 8 (over y, x, core).
Axes of the slice: x: 2, y: 2, z: 4, core: 2. Of those that a mesh axis runs over, the one named last changes fastest.
Arguments:
- gate_pre: bfloat16 [768, 14336], P('dp', 'mp'), may hold values from -8 to 8
- up_pre: bfloat16 [768, 14336], P('dp', 'mp'), may hold values from -6 to 6
- d_out: bfloat16 [768, 4096], P(('dp', 'mp')), may hold values from -6 to 6
- down_weight: bfloat16 [4096, 14336], P('dp', 'mp'), may hold values from -0.046875 to 0.046875
Outputs:
- d_gate: bfloat16 [768, 14336], P('dp', 'mp')
- d_up: bfloat16 [768, 14336], P('dp', 'mp')
- grad_down: bfloat16 [4096, 14336], P('dp', 'mp')
All inputs are finite; a program needn't handle non-finite values.
Results may differ from a plain program's by a relative error of at most 0.0095.
Values may be sent and summed in bfloat16 or wider, within the bound.
A program may use at most 128 MiB of HBM per device.

v0:
```python
import jax
import jax.numpy as jnp
from jax import lax
from jax.sharding import PartitionSpec as P


def body(gate_pre, up_pre, d_out, down_weight):
    gate = gate_pre.astype(jnp.float32)
    upper = up_pre.astype(jnp.float32)
    sig = jax.nn.sigmoid(gate)
    act = gate * sig
    hidden = (act * upper).astype(jnp.bfloat16)
    replicas = lax.axis_size("dp")
    full_out = lax.all_gather(d_out, "mp", axis=0, tiled=True)
    tok_rows = full_out.shape[0]
    local_hidden = hidden.shape[1]
    columns = full_out
    d_hidden = jnp.dot(
        columns,
        lax.all_gather(down_weight, "dp", axis=0, tiled=True),
        preferred_element_type=jnp.float32,
    )
    d_up = (d_hidden * act).astype(jnp.bfloat16)
    d_gate = (d_hidden * upper * sig * (1.0 + gate * (1.0 - sig))).astype(jnp.bfloat16)
    feature_rows = down_weight.shape[0]
    moved = lax.all_to_all(full_out, "dp", split_axis=1, concat_axis=0, tiled=True)
    piece = lax.all_gather(hidden, "dp", axis=0, tiled=True)
    blocks = piece.shape[0] // tok_rows
    columns = moved
    terms = jnp.einsum(
        "rtd,rtf->rdf",
        columns.reshape(blocks, tok_rows, feature_rows),
        piece.reshape(blocks, tok_rows, local_hidden),
        preferred_element_type=jnp.float32,
    )
    total = jnp.sum(terms.astype(jnp.bfloat16).astype(jnp.float32), axis=0)
    grad_down = (total / replicas).astype(jnp.bfloat16)
    return (d_gate, d_up, grad_down)


def solution(mesh):
    in_specs = (P("dp", "mp"), P("dp", "mp"), P(("dp", "mp"), None), P("dp", "mp"))
    out_specs = (P("dp", "mp"), P("dp", "mp"), P("dp", "mp"))
    return jax.shard_map(body, mesh=mesh, in_specs=in_specs, out_specs=out_specs, check_vma=False)
```

profile of v0, /device:TPU:0, one launch (start us, length us, event | category | flops | bytes accessed | tf_op | source)
XLA Modules:
  0.0 415.6 jit_solution(11324991727766426773)
XLA Ops:
  7.2 0.0 all-gather.4.cloned.1.call-start
  7.2 0.7 all-gather.4.cloned.1.call-update
  7.9 0.0 copy-start.1
  7.9 0.0 copy-start.2
  7.9 0.0 all-gather.6.cloned.1.call-start
  8.0 0.7 all-gather.6.cloned.1.call-update
  8.7 0.0 all-gather.8.cloned.1.call-start
  8.7 29.6 %all-gather.4.cloned.1.call-done = bf16[192,4096]{1,0:T(8,128)(2,1)} async-done(((bf16[24,4096]{1,0:T(8,128)(2,1)}), bf16[192,4096]{1,0:T(8,128)(2,1)}) %all-gather.4.cloned.1.call-update) | async-done | bytes 1572880 | tf_op jit(solution)/shard_map/all_gather | solution.py:14
  38.3 254.1 %all-gather.6.cloned.1.call-done = bf16[4096,1792]{1,0:T(8,128)(2,1)} async-done(((bf16[1024,1792]{1,0:T(8,128)(2,1)}), bf16[4096,1792]{1,0:T(8,128)(2,1)}) %all-gather.6.cloned.1.call-update) | async-done | bytes 14680080 | tf_op jit(solution)/shard_map/all_gather | solution.py:20
  292.4 0.0 copy-done.1
  292.4 0.0 copy-done.2
  292.4 0.0 copy-start
  292.4 10.4 %multiply_convert_fusion.1 = (bf16[192,1792]{1,0:T(8,128)(2,1)}, bf16[192,1792]{1,0:T(8,128)(2,1)}, bf16[192,1792]{1,0:T(8,128)(2,1)}) fusion(bf16[192,1792]{1,0:T(8,128)(2,1)S(1)} %copy-done.1, bf16[192,1792]{1,0:T(8,128)(2,1)S(1)} %copy-done.2, bf16[192,4096]{1,0:T(8,128)(2,1)} %all-gather.4.cloned.1.call-done, ...), kind=kOutput, calls=%fused_computation.18 | convolution fusion | flops 2824421376 | bytes 19693568 | tf_op jit(solution)/shard_map/dot_general | solution.py:18
  302.8 0.0 all-gather.8.cloned.1.call-update
  302.8 0.0 copy-done
  302.8 0.1 copy.12
  303.0 77.7 %all_to_all.16 = bf16[192,4,1024]{2,0,1:T(8,128)(2,1)S(1)} all-to-all(bf16[192,4,1024]{2,0,1:T(8,128)(2,1)S(1)} %bitcast.13), channel_id=1, replica_groups=mesh['dp'=4,'mp'=8] {'dp'}, dimensions={1} | all-to-all | bytes 3145728 | tf_op jit(solution)/shard_map/all_to_all | solution.py:26
  380.6 6.8 %all-gather.8.cloned.1.call-done = bf16[768,1792]{1,0:T(8,128)(2,1)} async-done(((bf16[192,1792]{1,0:T(8,128)(2,1)}), bf16[768,1792]{1,0:T(8,128)(2,1)}) %all-gather.8.cloned.1.call-update) | async-done | bytes 2752528 | tf_op jit(solution)/shard_map/all_gather | solution.py:27
  387.5 9.6 %convert_reduce_fusion = f32[1792,1024]{1,0:T(8,128)} fusion(bf16[4,192,1792]{2,1,0:T(8,128)(2,1)} %bitcast.15, bf16[192,4,1024]{2,0,1:T(8,128)(2,1)S(1)} %all_to_all.16), kind=kOutput, calls=%fused_computation | convolution fusion | flops 2838757376 | bytes 11665408 | tf_op jit(solution)/shard_map/rtd,rtf->rdf/dot_general | solution.py:30
  397.0 6.1 %fusion = bf16[1024,1792]{0,1:T(8,128)(2,1)} fusion(f32[1792,1024]{1,0:T(8,128)} %convert_reduce_fusion), kind=kLoop, calls=%fused_computation.2 | loop fusion | flops 3670016 | bytes 11010048 | tf_op jit(solution)/shard_map/convert_element_type | solution.py:37
  403.1 5.9 %copy.9 = bf16[1024,1792]{1,0:T(8,128)(2,1)} copy(bf16[1024,1792]{0,1:T(8,128)(2,1)} %fusion) | data formatting | bytes 7340032
Async XLA Ops:
  7.2 31.1 %all-gather.4.cloned.1.call-start = ((), (), s32[]{:S(2)}) async-start(), calls=%async_computation.1 | async-start | bytes 1769472 | tf_op jit(solution)/shard_map/all_gather | solution.py:14
  7.9 284.5 %copy-start.1 = (bf16[192,1792]{1,0:T(8,128)(2,1)S(1)}, bf16[192,1792]{1,0:T(8,128)(2,1)}, u32[]{:S(2)}) copy-start(bf16[192,1792]{1,0:T(8,128)(2,1)} %param.4) | copy-start | bytes 2064388
  7.9 284.5 %copy-start.2 = (bf16[192,1792]{1,0:T(8,128)(2,1)S(1)}, bf16[192,1792]{1,0:T(8,128)(2,1)}, u32[]{:S(2)}) copy-start(bf16[192,1792]{1,0:T(8,128)(2,1)} %param.5) | copy-start | bytes 2064388
  7.9 284.5 %all-gather.6.cloned.1.call-start = ((), (), s32[]{:S(2)}) async-start(), calls=%async_computation.2 | async-start | bytes 18350080 | tf_op jit(solution)/shard_map/all_gather | solution.py:20
  8.7 378.8 %all-gather.8.cloned.1.call-start = ((), (), s32[]{:S(2)}) async-start(), calls=%async_computation.3 | async-start | bytes 3440640 | tf_op jit(solution)/shard_map/all_gather | solution.py:27
  292.4 10.4 %copy-start = (bf16[192,4096]{1,0:T(8,128)(2,1)S(1)}, bf16[192,4096]{1,0:T(8,128)(2,1)}, u32[]{:S(2)}) copy-start(bf16[192,4096]{1,0:T(8,128)(2,1)} %all-gather.4.cloned.1.call-done) | copy-start | bytes 4718596
Sparse Core Ops, SparseCore 0:
  9.9 28.3 all-gather.3
  39.9 252.4 all-gather.5
  302.9 84.5 all-gather.7
where the time goes:
time: 416 us
  waiting for transfers between devices  292 us (70%)
  blocking collectives  77.7 us (19%)
  matrix products  19.9 us (5%)
  between operations  13.8 us (3%)
  other arithmetic  6.09 us (1%)
  local copies, waits for them, and re-layouts  6.06 us (1%)
    all_gather x1, waiting for transfers between devices, body(): lax.all_gather(down_weight, 'dp', axis=0, tiled=True)  254 us
    all_to_all x1, blocking collectives, body(): lax.all_to_all(full_out, 'dp', split_axis=1, concat_axis=0, tiled=True)  77.7 us
    all_gather x1, waiting for transfers between devices, body(): full_out = lax.all_gather(d_out, 'mp', axis=0, tiled=True)  29.6 us
    dot_general x1, matrix products, body(): jnp.dot(columns, lax.all_gather(down_weight, 'dp', axis=0, tiled=True), p...  10.4 us
    dot_general x1, matrix products, body(): jnp.einsum('rtd,rtf->rdf', columns.reshape(blocks, tok_rows, feature_rows...  9.56 us
  transfers between devices with their start and end apart: 3, of which 3 were waited for; matrix products, arithmetic and copies ran while one was open for 0% of the time, Pallas kernels for 0%

commit v1 on v0

--- a/solution.py
+++ b/solution.py
@@ -11,7 +11,12 @@
     act = gate * sig
     hidden = (act * upper).astype(jnp.bfloat16)
     replicas = lax.axis_size("dp")
-    full_out = lax.all_gather(d_out, "mp", axis=0, tiled=True)
+    ring = [d_out]
+    for hop in range(7):
+        ring.append(lax.ppermute(ring[-1], "mp", [(dev, (dev + 1) % 8) for dev in range(8)]))
+    full_out = jnp.roll(
+        jnp.concatenate(ring[::-1], axis=0), (lax.axis_index("mp") + 1) * ring[0].shape[0], axis=0
+    )
     tok_rows = full_out.shape[0]
     local_hidden = hidden.shape[1]
     columns = full_out

time: 416 us -> 381 us (0.916)
  waiting for transfers between devices: 292 us -> 263 us
  local copies, waits for them, and re-layouts: 6.06 us -> 0.92 us
    ppermute x0 -> x7, waiting for transfers between devices: none -> 42.2 us  [body(): lax.ppermute(ring[-1], 'mp', [(dev, (dev + 1) % 8) for dev in range(8)])]
    all_gather x1, waiting for transfers between devices: 254 us -> 213 us  [body(): lax.all_gather(down_weight, 'dp', axis=0, tiled=True)]
    all_gather x1 -> x0, waiting for transfers between devices: 29.6 us -> none  [body(): full_out = lax.all_gather(d_out, 'mp', axis=0, tiled=True)]
    unnamed x7 -> x21, local copies, waits for them, and re-layouts: 5.92 us -> 0.38 us
  transfers between devices with their start and end apart: 3 -> 9, of which waited for: 3 -> 9; matrix products, arithmetic and copies ran while one was open for 0% -> 0% of each run, Pallas kernels for 0% -> 0%
where the time goes in v1:
time: 381 us
  waiting for transfers between devices  263 us (69%)
  blocking collectives  77.7 us (20%)
  matrix products  19.3 us (5%)
  between operations  14.2 us (4%)
  other arithmetic  5.48 us (1%)
    all_gather x1, waiting for transfers between devices, body(): lax.all_gather(down_weight, 'dp', axis=0, tiled=True)  213 us
    all_to_all x1, blocking collectives, body(): lax.all_to_all(full_out, 'dp', split_axis=1, concat_axis=0, tiled=True)  77.7 us
    ppermute x7, waiting for transfers between devices, body(): lax.ppermute(ring[-1], 'mp', [(dev, (dev + 1) % 8) for dev in range(8)])  42.2 us
    dot_general x1, matrix products, body(): jnp.dot(columns, lax.all_gather(down_weight, 'dp', axis=0, tiled=True), p...  9.78 us
    dot_general x1, matrix products, body(): jnp.einsum('rtd,rtf->rdf', columns.reshape(blocks, tok_rows, feature_rows...  9.5 us
  transfers between devices with their start and end apart: 9, of which 9 were waited for; matrix products, arithmetic and copies ran while one was open for 0% of the time, Pallas kernels for 0%

profile of v1, /device:TPU:0, one launch (start us, length us, event | category | flops | bytes accessed | tf_op | source)
XLA Modules:
  0.0 381.1 jit_solution(1216410124087300782)
XLA Ops:
  7.2 0.0 copy-start
  7.2 0.0 all-gather.3.cloned.1.call-start
  7.2 0.7 all-gather.3.cloned.1.call-update
  7.9 0.0 all-gather.5.cloned.1.call-start
  8.0 0.1 copy-done
  8.1 0.5 collective-permute-start
  8.5 6.2 %collective-permute-done = bf16[24,4096]{1,0:T(8,128)(2,1)S(1)} collective-permute-done((bf16[24,4096]{1,0:T(8,128)(2,1)S(1)}, bf16[24,4096]{1,0:T(8,128)(2,1)S(1)}, u32[]{:S(2)}, u32[]{:S(2)}) %collective-permute-start) | collective-permute-done | bytes 196640 | tf_op jit(solution)/shard_map/ppermute | solution.py:16
  14.8 0.0 collective-permute-start.1
  14.8 6.0 %collective-permute-done.1 = bf16[24,4096]{1,0:T(8,128)(2,1)S(1)} collective-permute-done((bf16[24,4096]{1,0:T(8,128)(2,1)S(1)}, bf16[24,4096]{1,0:T(8,128)(2,1)S(1)}, u32[]{:S(2)}, u32[]{:S(2)}) %collective-permute-start.1) | collective-permute-done | bytes 196640 | tf_op jit(solution)/shard_map/ppermute | solution.py:16
  20.8 0.0 collective-permute-start.2
  20.8 6.0 %collective-permute-done.2 = bf16[24,4096]{1,0:T(8,128)(2,1)S(1)} collective-permute-done((bf16[24,4096]{1,0:T(8,128)(2,1)S(1)}, bf16[24,4096]{1,0:T(8,128)(2,1)S(1)}, u32[]{:S(2)}, u32[]{:S(2)}) %collective-permute-start.2) | collective-permute-done | bytes 196640 | tf_op jit(solution)/shard_map/ppermute | solution.py:16
  26.8 0.0 collective-permute-start.3
  26.8 6.0 %collective-permute-done.3 = bf16[24,4096]{1,0:T(8,128)(2,1)S(1)} collective-permute-done((bf16[24,4096]{1,0:T(8,128)(2,1)S(1)}, bf16[24,4096]{1,0:T(8,128)(2,1)S(1)}, u32[]{:S(2)}, u32[]{:S(2)}) %collective-permute-start.3) | collective-permute-done | bytes 196640 | tf_op jit(solution)/shard_map/ppermute | solution.py:16
  32.8 0.0 collective-permute-start.4
  32.8 6.0 %collective-permute-done.4 = bf16[24,4096]{1,0:T(8,128)(2,1)S(1)} collective-permute-done((bf16[24,4096]{1,0:T(8,128)(2,1)S(1)}, bf16[24,4096]{1,0:T(8,128)(2,1)S(1)}, u32[]{:S(2)}, u32[]{:S(2)}) %collective-permute-start.4) | collective-permute-done | bytes 196640 | tf_op jit(solution)/shard_map/ppermute | solution.py:16
  38.8 0.0 collective-permute-start.5
  38.8 6.0 %collective-permute-done.5 = bf16[24,4096]{1,0:T(8,128)(2,1)S(1)} collective-permute-done((bf16[24,4096]{1,0:T(8,128)(2,1)S(1)}, bf16[24,4096]{1,0:T(8,128)(2,1)S(1)}, u32[]{:S(2)}, u32[]{:S(2)}) %collective-permute-start.5) | collective-permute-done | bytes 196640 | tf_op jit(solution)/shard_map/ppermute | solution.py:16
  44.8 0.0 collective-permute-start.6
  44.8 6.0 %collective-permute-done.6 = bf16[24,4096]{1,0:T(8,128)(2,1)S(1)} collective-permute-done((bf16[24,4096]{1,0:T(8,128)(2,1)S(1)}, bf16[24,4096]{1,0:T(8,128)(2,1)S(1)}, u32[]{:S(2)}, u32[]{:S(2)}) %collective-permute-start.6) | collective-permute-done | bytes 196640 | tf_op jit(solution)/shard_map/ppermute | solution.py:16
  50.9 0.0 copy-start.1
  50.9 0.0 copy-start.2
  51.1 0.4 constant_dynamic-slice_fusion
  51.5 213.3 %all-gather.3.cloned.1.call-done = bf16[4096,1792]{1,0:T(8,128)(2,1)} async-done(((bf16[1024,1792]{1,0:T(8,128)(2,1)}), bf16[4096,1792]{1,0:T(8,128)(2,1)}) %all-gather.3.cloned.1.call-update) | async-done | bytes 14680080 | tf_op jit(solution)/shard_map/all_gather | solution.py:25
  264.8 0.0 copy-done.1
  264.8 0.0 copy-done.2
  264.8 9.8 %multiply_convert_fusion.1 = (bf16[192,1792]{1,0:T(8,128)(2,1)}, bf16[192,1792]{1,0:T(8,128)(2,1)}, bf16[192,1792]{1,0:T(8,128)(2,1)}) fusion(bf16[192,1792]{1,0:T(8,128)(2,1)S(1)} %copy-done.1, bf16[192,1792]{1,0:T(8,128)(2,1)S(1)} %copy-done.2, bf16[192,4096]{1,0:T(8,128)(2,1)S(1)} %constant_dynamic-slice_fusion, ...), kind=kOutput, calls=%fused_computation.17 | convolution fusion | flops 2824421376 | bytes 19693568 | tf_op jit(solution)/shard_map/dot_general | solution.py:23
  274.6 0.0 all-gather.5.cloned.1.call-update
  274.6 0.1 copy.10
  274.8 77.7 %all_to_all.16 = bf16[192,4,1024]{2,0,1:T(8,128)(2,1)S(1)} all-to-all(bf16[192,4,1024]{2,0,1:T(8,128)(2,1)S(1)} %bitcast.11), channel_id=1, replica_groups=mesh['dp'=4,'mp'=8] {'dp'}, dimensions={1} | all-to-all | bytes 3145728 | tf_op jit(solution)/shard_map/all_to_all | solution.py:31
  352.4 6.8 %all-gather.5.cloned.1.call-done = bf16[768,1792]{1,0:T(8,128)(2,1)} async-done(((bf16[192,1792]{1,0:T(8,128)(2,1)}), bf16[768,1792]{1,0:T(8,128)(2,1)}) %all-gather.5.cloned.1.call-update) | async-done | bytes 2752528 | tf_op jit(solution)/shard_map/all_gather | solution.py:32
  359.3 9.5 %convert_reduce_fusion = f32[1024,1792]{1,0:T(8,128)} fusion(bf16[4,192,1792]{2,1,0:T(8,128)(2,1)} %bitcast.13, bf16[192,4,1024]{2,0,1:T(8,128)(2,1)S(1)} %all_to_all.16), kind=kOutput, calls=%fused_computation | convolution fusion | flops 2838757376 | bytes 11665408 | tf_op jit(solution)/shard_map/rtd,rtf->rdf/dot_general | solution.py:35
  368.8 5.5 %multiply_convert_fusion = bf16[1024,1792]{1,0:T(8,128)(2,1)} fusion(f32[1024,1792]{1,0:T(8,128)} %convert_reduce_fusion), kind=kLoop, calls=%fused_computation.1 | loop fusion | flops 3670016 | bytes 11010048 | tf_op jit(solution)/shard_map/convert_element_type | solution.py:42
  (16 shorter events, 0.2 us)
Async XLA Ops:
  7.2 0.9 copy-start
  7.2 257.6 %all-gather.3.cloned.1.call-start = ((), (), s32[]{:S(2)}) async-start(), calls=%async_computation.1 | async-start | bytes 18350080 | tf_op jit(solution)/shard_map/all_gather | solution.py:25
  7.9 351.4 %all-gather.5.cloned.1.call-start = ((), (), s32[]{:S(2)}) async-start(), calls=%async_computation.2 | async-start | bytes 3440640 | tf_op jit(solution)/shard_map/all_gather | solution.py:32
  8.1 6.7 %collective-permute-start = (bf16[24,4096]{1,0:T(8,128)(2,1)S(1)}, bf16[24,4096]{1,0:T(8,128)(2,1)S(1)}, u32[]{:S(2)}, u32[]{:S(2)}) collective-permute-start(bf16[24,4096]{1,0:T(8,128)(2,1)S(1)} %copy-done), channel_id=1, source_target_pairs={{0,1},{1,2},{2,3},{3,4},{4,5},{5,6},{6,7},{7,0},{8,9},{9,10},{10,1... | collective-permute-start | bytes 589832 | tf_op jit(solution)/shard_map/ppermute | solution.py:16
  14.8 6.0 %collective-permute-start.1 = (bf16[24,4096]{1,0:T(8,128)(2,1)S(1)}, bf16[24,4096]{1,0:T(8,128)(2,1)S(1)}, u32[]{:S(2)}, u32[]{:S(2)}) collective-permute-start(bf16[24,4096]{1,0:T(8,128)(2,1)S(1)} %collective-permute-done), channel_id=1, source_target_pairs={{0,1},{1,2},{2,3},{3,4},{4,5},{5,6},{6,7},{7,0},{8,9},{9,10},{10,1... | collective-permute-start | bytes 589832 | tf_op jit(solution)/shard_map/ppermute | solution.py:16
  20.8 6.0 %collective-permute-start.2 = (bf16[24,4096]{1,0:T(8,128)(2,1)S(1)}, bf16[24,4096]{1,0:T(8,128)(2,1)S(1)}, u32[]{:S(2)}, u32[]{:S(2)}) collective-permute-start(bf16[24,4096]{1,0:T(8,128)(2,1)S(1)} %collective-permute-done.1), channel_id=1, source_target_pairs={{0,1},{1,2},{2,3},{3,4},{4,5},{5,6},{6,7},{7,0},{8,9},{9,10},{10,1... | collective-permute-start | bytes 589832 | tf_op jit(solution)/shard_map/ppermute | solution.py:16
  26.8 6.0 %collective-permute-start.3 = (bf16[24,4096]{1,0:T(8,128)(2,1)S(1)}, bf16[24,4096]{1,0:T(8,128)(2,1)S(1)}, u32[]{:S(2)}, u32[]{:S(2)}) collective-permute-start(bf16[24,4096]{1,0:T(8,128)(2,1)S(1)} %collective-permute-done.2), channel_id=1, source_target_pairs={{0,1},{1,2},{2,3},{3,4},{4,5},{5,6},{6,7},{7,0},{8,9},{9,10},{10,1... | collective-permute-start | bytes 589832 | tf_op jit(solution)/shard_map/ppermute | solution.py:16
  32.8 6.0 %collective-permute-start.4 = (bf16[24,4096]{1,0:T(8,128)(2,1)S(1)}, bf16[24,4096]{1,0:T(8,128)(2,1)S(1)}, u32[]{:S(2)}, u32[]{:S(2)}) collective-permute-start(bf16[24,4096]{1,0:T(8,128)(2,1)S(1)} %collective-permute-done.3), channel_id=1, source_target_pairs={{0,1},{1,2},{2,3},{3,4},{4,5},{5,6},{6,7},{7,0},{8,9},{9,10},{10,1... | collective-permute-start | bytes 589832 | tf_op jit(solution)/shard_map/ppermute | solution.py:16
  38.8 6.0 %collective-permute-start.5 = (bf16[24,4096]{1,0:T(8,128)(2,1)S(1)}, bf16[24,4096]{1,0:T(8,128)(2,1)S(1)}, u32[]{:S(2)}, u32[]{:S(2)}) collective-permute-start(bf16[24,4096]{1,0:T(8,128)(2,1)S(1)} %collective-permute-done.4), channel_id=1, source_target_pairs={{0,1},{1,2},{2,3},{3,4},{4,5},{5,6},{6,7},{7,0},{8,9},{9,10},{10,1... | collective-permute-start | bytes 589832 | tf_op jit(solution)/shard_map/ppermute | solution.py:16
  44.8 6.0 %collective-permute-start.6 = (bf16[24,4096]{1,0:T(8,128)(2,1)S(1)}, bf16[24,4096]{1,0:T(8,128)(2,1)S(1)}, u32[]{:S(2)}, u32[]{:S(2)}) collective-permute-start(bf16[24,4096]{1,0:T(8,128)(2,1)S(1)} %collective-permute-done.5), channel_id=1, source_target_pairs={{0,1},{1,2},{2,3},{3,4},{4,5},{5,6},{6,7},{7,0},{8,9},{9,10},{10,1... | collective-permute-start | bytes 589832 | tf_op jit(solution)/shard_map/ppermute | solution.py:16
  50.9 213.9 %copy-start.1 = (bf16[192,1792]{1,0:T(8,128)(2,1)S(1)}, bf16[192,1792]{1,0:T(8,128)(2,1)}, u32[]{:S(2)}) copy-start(bf16[192,1792]{1,0:T(8,128)(2,1)} %param.4) | copy-start | bytes 2064388
  50.9 213.9 %copy-start.2 = (bf16[192,1792]{1,0:T(8,128)(2,1)S(1)}, bf16[192,1792]{1,0:T(8,128)(2,1)}, u32[]{:S(2)}) copy-start(bf16[192,1792]{1,0:T(8,128)(2,1)} %param.5) | copy-start | bytes 2064388
Sparse Core Ops, SparseCore 0:
  9.6 255.1 all-gather.2
  274.7 84.4 all-gather.4
